TPU v7x, 256 devices: a whole 4x4x8 slice. The times are simulated.
256 devices in a mesh: seq: 64 (over z, x, core), tp: 4 (over y).
Axes of the slice: x: 4, y: 4, z: 8, core: 2. Of those that a mesh axis runs over, the one named last changes fastest.
Arguments:
- prompt_keys: bfloat16 [64, 16384, 512], P(None, 'seq', 'tp'), may hold values from -6 to 16
- prompt_values: bfloat16 [64, 16384, 512], P(None, 'seq', 'tp'), may hold values from -6 to 6
- keep_mask: int32 [64, 128, 4], P(None, 'seq', 'tp'), may hold values from 0 to 1, as said below
- owner_sequence: int32 [64], replicated, may hold values from 0 to 63, each once
- step_queries: bfloat16 [64, 16, 4, 1024], P('seq', None, 'tp'), may hold values from -15 to 26
- new_keys: bfloat16 [64, 16, 512], P('seq', None, 'tp'), may hold values from -12 to 12
- new_values: bfloat16 [64, 16, 512], P('seq', None, 'tp'), may hold values from -6 to 6
Outputs:
- attended: bfloat16 [64, 16, 4, 1024], P('seq', None, 'tp')
Inputs may be any that keep to these rules, and one draw needn't show every extreme that they name: `keep_mask`: the last block of every sequence is kept for every head; every sequence and head keeps between 32 and 96 blocks.
All inputs are finite; a program needn't handle non-finite values.
Results may differ from a plain program's by a relative error of at most 0.009.
The roundings to bfloat16 on the way count: a program that leaves them out, or rounds other values in their place, can miss the bound.
Values may be sent and summed in bfloat16 or wider, within the bound.
A program may use at most 128 MiB of HBM per device.

v0:
```python
import math

import jax
import jax.numpy as jnp
from jax import lax
from jax.sharding import PartitionSpec as P

KEEP = 96


floor_score = -1e30


def frequencies(half_width):
    position_index = jnp.arange(half_width).astype(jnp.float32)
    base_rate = jnp.exp(position_index * (-2.0 / (2 * half_width)) * math.log(500000.0))
    wavelength = 2.0 * math.pi / base_rate
    smooth = (8192.0 / wavelength - 1.0) / 3.0
    blended = (1.0 - smooth) * base_rate / 8.0 + smooth * base_rate
    return jnp.where(
        wavelength < 2048.0, base_rate, jnp.where(wavelength > 8192.0, base_rate / 8.0, blended)
    )


def rotate(vector, offset):
    half_width = vector.shape[-1] // 2
    angles = offset.astype(jnp.float32)[..., None] * frequencies(half_width)
    cosine = jnp.cos(angles)
    sine_part = jnp.sin(angles)
    lower_half = vector[..., :half_width]
    upper_half = vector[..., half_width:]
    return jnp.concatenate(
        [
            lower_half * cosine - upper_half * sine_part,
            upper_half * cosine + lower_half * sine_part,
        ],
        axis=-1,
    )


def select_blocks(mask_column, block_size):
    running = jnp.cumsum(mask_column)
    slot_index = jnp.arange(KEEP)
    chosen = jnp.sum((running[None, :] <= slot_index[:, None]).astype(jnp.int32), axis=1)
    chosen = jnp.minimum(chosen, mask_column.shape[0] - 1)
    live_slots = slot_index < running[-1]
    return (chosen, live_slots, (slot_index - chosen) * block_size)


def attend(query_rows, cached_keys, cached_values, live_tokens, fresh_keys, fresh_values, groups):
    score_scale = 1.0 / math.sqrt(query_rows.shape[-1])
    older = jnp.dot(query_rows, cached_keys.T, preferred_element_type=jnp.float32) * score_scale
    older = jnp.where(live_tokens[None, :], older, floor_score)
    new_scores = jnp.dot(query_rows, fresh_keys.T, preferred_element_type=jnp.float32) * score_scale
    row_step = jnp.arange(query_rows.shape[0]) // groups
    causal = row_step[:, None] >= jnp.arange(fresh_keys.shape[0])[None, :]
    new_scores = jnp.where(causal, new_scores, floor_score)
    highest = jnp.maximum(jnp.max(older, axis=1), jnp.max(new_scores, axis=1))
    older_weight = jnp.where(live_tokens[None, :], jnp.exp(older - highest[:, None]), 0.0)
    newer_weight = jnp.where(causal, jnp.exp(new_scores - highest[:, None]), 0.0)
    row_total = jnp.sum(older_weight, axis=1) + jnp.sum(newer_weight, axis=1)
    result = jnp.dot(
        (older_weight / row_total[:, None]).astype(jnp.bfloat16),
        cached_values,
        preferred_element_type=jnp.float32,
    )
    result = result + jnp.dot(
        (newer_weight / row_total[:, None]).astype(jnp.bfloat16),
        fresh_values,
        preferred_element_type=jnp.float32,
    )
    return result


def shards(
    prompt_keys, prompt_values, keep_mask, owner_sequence, step_queries, new_keys, new_values
):
    sequences, tokens_here, columns = prompt_keys.shape
    heads_here = keep_mask.shape[2]
    blocks_here = keep_mask.shape[1]
    head_width = columns // heads_here
    block_size = tokens_here // blocks_here
    owners = lax.axis_size("seq")
    step_count = step_queries.shape[1]
    groups = step_queries.shape[3] // head_width
    query_all = step_queries[0].reshape(step_count, heads_here, groups, head_width)
    fresh_all = new_keys[0].reshape(step_count, heads_here, head_width)
    fresh_vals = new_values[0].reshape(step_count, heads_here, head_width)
    step_index = jnp.arange(step_count)
    outgoing = (
        jnp.take(prompt_keys, owner_sequence, axis=0),
        jnp.take(prompt_values, owner_sequence, axis=0),
        jnp.take(keep_mask, owner_sequence, axis=0).astype(jnp.bfloat16),
    )
    got_keys, got_values, got_mask = (
        lax.all_to_all(outgoing[0], "seq", split_axis=0, concat_axis=0, tiled=True),
        lax.all_to_all(outgoing[1], "seq", split_axis=0, concat_axis=0, tiled=True),
        lax.all_to_all(outgoing[2], "seq", split_axis=0, concat_axis=0, tiled=True),
    )
    total_blocks = owners * blocks_here
    key_blocks = got_keys.reshape(total_blocks, block_size, heads_here, head_width)
    value_blocks = got_values.reshape(total_blocks, block_size, heads_here, head_width)
    mask_rows = (got_mask > 0.5).astype(jnp.int32).reshape(total_blocks, heads_here)
    counts = jnp.sum(mask_rows, axis=0)
    longest = lax.pmax(jnp.max(counts), "tp")
    positions = longest * block_size + step_index
    chosen, live_slots, offset = select_blocks(mask_rows[:, 0], block_size)
    picked = jnp.take(key_blocks[:, :, 0], chosen, axis=0)
    turned = (
        rotate(picked.astype(jnp.float32), offset[:, None])
        .astype(jnp.bfloat16)
        .reshape(KEEP * block_size, head_width)
    )
    kept_values = jnp.take(value_blocks[:, :, 0], chosen, axis=0).reshape(
        KEEP * block_size, head_width
    )
    live_tokens = jnp.repeat(live_slots, block_size)
    query_rows = (
        rotate(query_all[:, 0].astype(jnp.float32), positions[:, None])
        .astype(jnp.bfloat16)
        .reshape(step_count * groups, head_width)
    )
    fresh_turned = rotate(fresh_all[:, 0].astype(jnp.float32), positions).astype(jnp.bfloat16)
    result = attend(
        query_rows, turned, kept_values, live_tokens, fresh_turned, fresh_vals[:, 0], groups
    )
    outputs = [result.reshape(step_count, groups * head_width)]
    return jnp.stack(outputs, axis=1)[None].astype(jnp.bfloat16)


def solution(mesh):
    in_specs = (
        P(None, "seq", "tp"),
        P(None, "seq", "tp"),
        P(None, "seq", "tp"),
        P(),
        P("seq", None, "tp", None),
        P("seq", None, "tp"),
        P("seq", None, "tp"),
    )
    out_specs = P("seq", None, "tp", None)
    return jax.shard_map(shards, mesh=mesh, in_specs=in_specs, out_specs=out_specs, check_vma=False)
```

profile of v0, /device:TPU:1, one launch (start us, length us, event | category | flops | bytes accessed | tf_op | source)
XLA Modules:
  0.0 256.7 jit_solution(10231161319348646731)
XLA Ops:
  0.0 0.7 compare_select_fusion.1
  0.7 0.7 compare_and_fusion.1
  1.3 0.8 copy.20
  2.1 0.6 gather_fusion
  2.8 0.7 copy.22
  3.5 13.0 %all-to-all-start = ((bf16[64,2,1]{1,2,0:T(2,128)(2,1)}), bf16[64,2,1]{1,2,0:T(2,128)(2,1)S(1)}, u32[]{:S(2)}, u32[]{:S(2)}) async-start(bf16[64,2,1]{1,2,0:T(2,128)(2,1)} %copy.22), calls=%async_computation | async-start | bytes 65536 | tf_op jit(solution)/shard_map/all_to_all | solution.py:98
  16.5 5.2 %gather_fusion.1 = bf16[64,256,128]{2,1,0:T(8,128)(2,1)} fusion(bf16[64,256,128]{2,1,0:T(8,128)(2,1)} %param.11, s32[1024]{0:T(1024)S(1)} %pad_clamp_fusion.1), kind=kCustom, calls=%fused_computation.clone | custom fusion | bytes 8388864 | tf_op jit(solution)/shard_map/jit(_take)/gather | solution.py:91
  21.7 5.2 %gather_fusion.3 = bf16[64,256,128]{2,1,0:T(8,128)(2,1)} fusion(bf16[64,256,128]{2,1,0:T(8,128)(2,1)} %param.12, s32[1024]{0:T(1024)S(1)} %pad_clamp_fusion.1), kind=kCustom, calls=%fused_computation.2.clone | custom fusion | bytes 8388864 | tf_op jit(solution)/shard_map/jit(_take)/gather | solution.py:92
  27.0 6.0 %broadcast_select_fusion.1 = (bf16[64,256,128]{2,1,0:T(8,128)(2,1)}, bf16[64,256,128]{2,1,0:T(8,128)(2,1)}) fusion(bf16[64,256,128]{2,1,0:T(8,128)(2,1)} %gather_fusion.1, pred[64]{0:T(512)(128)(4,1)S(1)} %compare_and_fusion.1, bf16[64,256,128]{2,1,0:T(8,128)(2,1)} %gather_fusion.3), kind=kLoop, calls=%fused_computation.13 | loop fusion | flops 4194304 | bytes 16777280 | tf_op jit(solution)/shard_map/jit(_take)/select_n | solution.py:91
  32.9 105.0 %all_to_all.15 = bf16[64,256,128]{2,1,0:T(8,128)(2,1)} all-to-all(bf16[64,256,128]{2,1,0:T(8,128)(2,1)} %get-tuple-element.23), channel_id=1, replica_groups=mesh['seq'=64,'tp'=4] {'seq'}, dimensions={0} | all-to-all | bytes 8388608 | tf_op jit(solution)/shard_map/all_to_all | solution.py:96
  138.0 7.3 %all-to-all-start.2 = ((bf16[64,256,128]{2,1,0:T(8,128)(2,1)}), bf16[64,256,128]{2,1,0:T(8,128)(2,1)}, u32[]{:S(2)}, u32[]{:S(2)}) async-start(bf16[64,256,128]{2,1,0:T(8,128)(2,1)} %get-tuple-element.24), calls=%async_computation.2 | async-start | bytes 8388608 | tf_op jit(solution)/shard_map/all_to_all | solution.py:97
  145.4 0.7 fusion.10
  146.1 8.5 %pmax.7 = s32[]{:T(128)} all-reduce(s32[]{:T(128)} %get-tuple-element.6), channel_id=1, replica_groups=mesh['seq'=64,'tp'=4] {'tp'}, use_global_device_ids=true, to_apply=%region_2.3 | all-reduce | flops 1 | bytes 8 | tf_op jit(solution)/shard_map/pmax | solution.py:105
  154.7 0.2 reduce-window.4
  154.8 0.1 reduce.3
  155.0 0.6 slice.39
  156.2 0.6 iota_compare_fusion.2
  156.8 0.1 convert_reduce_fusion
  156.9 0.1 subtract_convert_fusion.2
  157.1 0.1 fusion.8
  157.2 0.2 fusion.27
  157.4 0.3 multiply_cosine_fusion
  157.7 3.3 %gather_fusion.2 = bf16[96,128,128]{2,1,0:T(8,128)(2,1)S(1)} fusion(bf16[128,128,128]{2,1,0:T(8,128)(2,1)} %bitcast.30, s32[1024]{0:T(1024)S(1)} %pad_clamp_fusion), kind=kCustom, calls=%fused_computation.1.clone | custom fusion | bytes 6291840 | tf_op jit(solution)/shard_map/jit(_take)/gather | solution.py:108
  161.1 78.8 %all-to-all-done.2 = bf16[64,256,128]{2,1,0:T(8,128)(2,1)} async-done(((bf16[64,256,128]{2,1,0:T(8,128)(2,1)}), bf16[64,256,128]{2,1,0:T(8,128)(2,1)}, u32[]{:S(2)}, u32[]{:S(2)}) %all-to-all-start.2) | async-done | bytes 4194336 | tf_op jit(solution)/shard_map/all_to_all | solution.py:97
  239.9 4.9 %gather_fusion.4 = bf16[96,128,128]{2,1,0:T(8,128)(2,1)} fusion(bf16[128,128,128]{2,1,0:T(8,128)(2,1)} %bitcast.11, s32[1024]{0:T(1024)S(1)} %pad_clamp_fusion), kind=kCustom, calls=%fused_computation.3.clone | custom fusion | bytes 6291840 | tf_op jit(solution)/shard_map/jit(_take)/gather | solution.py:114
  244.8 2.8 %select_convert_fusion = (f32[96,128,128]{2,1,0:T(8,128)S(1)}, bf16[96,128,128]{2,1,0:T(8,128)(2,1)S(1)}) fusion(bf16[96,128,128]{2,1,0:T(8,128)(2,1)S(1)} %gather_fusion.2, pred[96]{0:T(512)(128)(4,1)S(1)} %get-tuple-element.9, bf16[96,128,128]{2,1,0:T(8,128)(2,1)} %gather_fusion.4), kind=kLoop, calls=%fused_computation.17 | loop fusion | flops 4718592 | bytes 15728736 | tf_op jit(solution)/shard_map/convert_element_type | solution.py:110
  247.6 2.6 %subtract_convert_fusion = (bf16[96,128,64]{2,1,0:T(8,128)(2,1)S(1)}, bf16[96,128,64]{2,1,0:T(8,128)(2,1)S(1)}) fusion(f32[96,128,128]{2,1,0:T(8,128)S(1)} %get-tuple-element.21, f32[96,64]{1,0:T(8,128)S(1)} %get-tuple-element.20, f32[96,64]{1,0:T(8,128)S(1)} %get-tuple-element.19), kind=kLoop, calls=%fused_computation.10 | loop fusion | flops 6291456 | bytes 9486336 | tf_op jit(solution)/shard_map/convert.7
  250.3 2.5 fusion.26
  252.8 1.4 fusion.1
  254.2 1.7 fusion.5
  255.9 0.2 fusion.6
  256.1 0.6 convert_element_type.109
  (24 shorter events, 0.4 us)
Async XLA Ops:
  0.0 255.9 %copy-start = (bf16[1,16,128]{2,1,0:T(8,128)(2,1)S(1)}, bf16[1,16,128]{2,1,0:T(8,128)(2,1)}, u32[]{:S(2)}) copy-start(bf16[1,16,128]{2,1,0:T(8,128)(2,1)} %param.17) | copy-start | bytes 12292
  3.5 29.4 %all-to-all-start = ((bf16[64,2,1]{1,2,0:T(2,128)(2,1)}), bf16[64,2,1]{1,2,0:T(2,128)(2,1)S(1)}, u32[]{:S(2)}, u32[]{:S(2)}) async-start(bf16[64,2,1]{1,2,0:T(2,128)(2,1)} %copy.22), calls=%async_computation | async-start | bytes 65536 | tf_op jit(solution)/shard_map/all_to_all | solution.py:98
  138.0 7.4 %copy-start.1 = (bf16[1,16,1,1024]{3,1,2,0:T(8,128)(2,1)S(1)}, bf16[1,16,1,1024]{3,1,2,0:T(8,128)(2,1)}, u32[]{:S(2)}) copy-start(bf16[1,16,1,1024]{3,1,2,0:T(8,128)(2,1)} %param.15) | copy-start | bytes 98308
  138.0 7.4 %copy-start.2 = (bf16[1,16,128]{2,1,0:T(8,128)(2,1)S(1)}, bf16[1,16,128]{2,1,0:T(8,128)(2,1)}, u32[]{:S(2)}) copy-start(bf16[1,16,128]{2,1,0:T(8,128)(2,1)} %param.16) | copy-start | bytes 12292
  138.0 101.9 %all-to-all-start.2 = ((bf16[64,256,128]{2,1,0:T(8,128)(2,1)}), bf16[64,256,128]{2,1,0:T(8,128)(2,1)}, u32[]{:S(2)}, u32[]{:S(2)}) async-start(bf16[64,256,128]{2,1,0:T(8,128)(2,1)} %get-tuple-element.24), calls=%async_computation.2 | async-start | bytes 8388608 | tf_op jit(solution)/shard_map/all_to_all | solution.py:97
where the time goes:
time: 258 us; the launch traced here: 257 us
  blocking collectives  113 us (44%)
  waiting for transfers between devices  78.8 us (31%)
  local copies, waits for them, and re-layouts  22.2 us (9%)
  starting transfers between devices  20.3 us (8%)
  other arithmetic  16.5 us (6%)
  matrix products  4.57 us (2%)
    all_to_all x1, blocking collectives, shards(): lax.all_to_all(outgoing[0], 'seq', split_axis=0, concat_axis=0, tiled=True)  105 us
    all_to_all x1, waiting for transfers between devices, shards(): lax.all_to_all(outgoing[1], 'seq', split_axis=0, concat_axis=0, tiled=True)  78.8 us
    all_to_all x1, starting transfers between devices, shards(): lax.all_to_all(outgoing[2], 'seq', split_axis=0, concat_axis=0, tiled=True)  13 us
    pmax x1, blocking collectives, shards(): longest = lax.pmax(jnp.max(counts), 'tp')  8.46 us
    all_to_all x1, starting transfers between devices, shards(): lax.all_to_all(outgoing[1], 'seq', split_axis=0, concat_axis=0, tiled=True)  7.34 us
    select_n x1, other arithmetic, shards(): jnp.take(prompt_keys, owner_sequence, axis=0)  5.95 us
    gather x1, local copies, waits for them, and re-layouts, shards(): jnp.take(prompt_values, owner_sequence, axis=0)  5.25 us
    gather x1, local copies, waits for them, and re-layouts, shards(): jnp.take(prompt_keys, owner_sequence, axis=0)  5.2 us
  transfers between devices with their start and end apart: 2, of which 1 were waited for; matrix products, arithmetic and copies ran while one was open for 9% of the time, Pallas kernels for 0%

commit v1 on v0

v1 whole, which is shorter than its diff:
```python
import functools
import math

import jax
import jax.numpy as jnp
from jax import lax
from jax.experimental import pallas as pl
from jax.experimental.pallas import tpu as pltpu
from jax.sharding import PartitionSpec as P

BLOCK = 128
HEAD = 128
NEG = -1e30
MESH = pl.DeviceIdType.MESH
F32 = jnp.float32
BF16 = jnp.bfloat16


def frequencies(half_width):
    position_index = jnp.arange(half_width).astype(jnp.float32)
    base_rate = jnp.exp(position_index * (-2.0 / (2 * half_width)) * math.log(500000.0))
    wavelength = 2.0 * math.pi / base_rate
    smooth = (8192.0 / wavelength - 1.0) / 3.0
    blended = (1.0 - smooth) * base_rate / 8.0 + smooth * base_rate
    return jnp.where(
        wavelength < 2048.0, base_rate, jnp.where(wavelength > 8192.0, base_rate / 8.0, blended)
    )


def kernel(
    nz, nx, ny,
    owner_ref, flags_ref, freq_ref, query_ref, newk_ref, newv_ref, keys_hbm, values_hbm,
    out_ref,
    keys, values, queries, counts, totals, table, live, pair_out, pair_in, pair_own,
    x_out, x_in, x_own, z_out, z_in, z_own,
    load_sem, c1_send, c1_recv, c2_send, c2_recv, t_send, t_recv,
    qz_send, qz_recv, qx_send, qx_recv, qc_send, qc_recv,
    pair_send, pair_recv, x_send, x_recv, z_send, z_recv,
):
    seqs = nz * nx * 2
    group = nx * 2
    tokens = 2 * BLOCK
    steps = newk_ref.shape[0]
    heads = query_ref.shape[1] // HEAD
    rows = steps * heads
    score_scale = math.log2(math.e) / math.sqrt(HEAD)

    me = lax.axis_index("seq")
    tp = lax.axis_index("tp")
    z = me // group
    x = (me // 2) % nx
    c = me % 2
    sib = 1 - c

    def dev(z_, x_, c_):
        return (z_ * nx + x_) * 2 + c_

    def far(i):
        half = nz // 2
        return (half + (i % 2) * (nz - (i + 1) // 2) + (1 - i % 2) * (i // 2)) % nz

    def remote(src, dst, send, recv, where, where_tp=None):
        return pltpu.make_async_remote_copy(
            src_ref=src, dst_ref=dst, send_sem=send, recv_sem=recv,
            device_id=(where, tp if where_tp is None else where_tp), device_id_type=MESH,
        )

    chunk = seqs // nz

    def load(i, which):
        src, dst = ((keys_hbm, keys), (values_hbm, values))[which]
        part = pl.ds(i * chunk, chunk)
        return pltpu.make_async_copy(src.at[part], dst.at[part], load_sem.at[which, i])

    for i in range(nz):
        load(i, 0).start()
        load(i, 1).start()

    counts[me] = flags_ref[0:1, :] + flags_ref[1:2, :]
    for g in range(heads):
        queries[me, g * steps:(g + 1) * steps, :] = query_ref[:, g * HEAD:(g + 1) * HEAD]

    barrier = pltpu.get_barrier_semaphore()
    near = z * group
    xc = x * 2 + c
    for r in range(1, group):
        pl.semaphore_signal(barrier, inc=1, device_id=(near + (xc + r) % group, tp), device_id_type=MESH)
    for d in range(1, nz):
        pl.semaphore_signal(barrier, inc=1, device_id=(dev((z + d) % nz, x, c), tp), device_id_type=MESH)
    for d in range(1, ny):
        pl.semaphore_signal(barrier, inc=1, device_id=(me, (tp + d) % ny), device_id_type=MESH)
    pl.semaphore_wait(barrier, group - 1 + nz - 1 + ny - 1)

    def counts_near(r):
        return remote(counts.at[me], counts.at[me], c1_send.at[r], c1_recv.at[r], near + (xc + r) % group)

    def counts_near_in(r):
        slot = near + (xc - r + group) % group
        return remote(counts.at[slot], counts.at[slot], c1_send.at[r], c1_recv.at[r], slot)

    def counts_far(d):
        part = pl.ds(z * group, group)
        return remote(counts.at[part], counts.at[part], c2_send.at[d], c2_recv.at[d], dev((z + d) % nz, x, c))

    def counts_far_in(d):
        z_ = (z - d + nz) % nz
        part = pl.ds(z_ * group, group)
        return remote(counts.at[part], counts.at[part], c2_send.at[d], c2_recv.at[d], dev(z_, x, c))

    def query_z(i):
        return remote(queries.at[me], queries.at[me], qz_send.at[i], qz_recv.at[i],
                      dev((z - far(i) + nz) % nz, x, c))

    def query_z_in(i):
        slot = dev((z + far(i)) % nz, x, c)
        return remote(queries.at[slot], queries.at[slot], qz_send.at[i], qz_recv.at[i], slot)

    def query_x(i, d):
        slot = dev((z + far(i)) % nz, x, c)
        return remote(queries.at[slot], queries.at[slot], qx_send.at[i, d], qx_recv.at[i, d],
                      dev(z, (x + d) % nx, c))

    def query_x_in(i, d):
        x_ = (x - d + nx) % nx
        slot = dev((z + far(i)) % nz, x_, c)
        return remote(queries.at[slot], queries.at[slot], qx_send.at[i, d], qx_recv.at[i, d], dev(z, x_, c))

    def query_c(i, d):
        slot = dev((z + far(i)) % nz, (x - d + nx) % nx, c)
        return remote(queries.at[slot], queries.at[slot], qc_send.at[i, d], qc_recv.at[i, d], dev(z, x, sib))

    def query_c_in(i, d):
        slot = dev((z + far(i)) % nz, (x - d + nx) % nx, sib)
        return remote(queries.at[slot], queries.at[slot], qc_send.at[i, d], qc_recv.at[i, d], dev(z, x, sib))

    def forward_z(i):
        for d in range(1, nx):
            query_x(i, d).start()
        query_c(i, 0).start()

    def forward_x(i):
        for d in range(1, nx):
            query_x_in(i, d).wait_recv()
            query_c(i, d).start()

    for r in range(1, group):
        counts_near(r).start()
    for i in range(nz - 1):
        query_z(i).start()
    for r in range(1, group):
        counts_near_in(r).wait_recv()
    for d in range(1, nz):
        counts_far(d).start()
    forward_z(nz - 1)
    for d in range(1, nz):
        counts_far_in(d).wait_recv()

    before = jnp.zeros((1, HEAD), F32)
    total = jnp.zeros((1, HEAD), F32)
    for j in range(seqs):
        row = counts[j]
        total = total + row
        before = before + jnp.where(j < me, row, 0.0)
    totals[tp] = total
    for d in range(1, ny):
        remote(totals.at[tp], totals.at[tp], t_send.at[d], t_recv.at[d], me, (tp + d) % ny).start()

    freq = freq_ref[...]
    lane = lax.broadcasted_iota(jnp.int32, (1, HEAD), 1)
    sign = jnp.where(lane < HEAD // 2, -1.0, 1.0).astype(F32)

    def down(row):
        return jnp.transpose(jnp.broadcast_to(row, (HEAD, HEAD)))[:seqs]

    slot0 = before
    slot1 = before + flags_ref[0:1, :]
    first_block = (2 * me).astype(F32)
    for j, slot in enumerate((slot0, slot1)):
        angle = (down(slot) - (first_block + j)) * float(BLOCK) * freq
        table[2 * j] = jnp.cos(angle)
        table[2 * j + 1] = jnp.sin(angle) * sign
        live[j] = down(flags_ref[j:j + 1, :])

    def rotate_keys(i, carry):
        for j in range(2):
            cosine = table[2 * j, pl.ds(i, 1), :]
            sine = table[2 * j + 1, pl.ds(i, 1), :]
            part = pl.ds(j * BLOCK, BLOCK)
            stored = keys[i, part, :].astype(F32)
            turned = stored * cosine + pltpu.roll(stored, HEAD // 2, 1) * sine
            keys[i, part, :] = turned.astype(BF16)
        return carry

    for i in range(nz):
        load(i, 0).wait()
        lax.fori_loop(i * chunk, (i + 1) * chunk, rotate_keys, 0)
        if i < nz - 1:
            query_z_in(i).wait_recv()
            forward_z(i)
    for i in range(nz):
        load(i, 1).wait()

    longest = total
    for d in range(1, ny):
        slot = (tp - d + ny) % ny
        remote(totals.at[slot], totals.at[slot], t_send.at[d], t_recv.at[d], me, slot).wait_recv()
    for d in range(1, ny):
        longest = jnp.maximum(longest, totals[(tp + d) % ny])
    angle = down(longest) * float(BLOCK) * freq
    table[4] = jnp.cos(angle)
    table[5] = jnp.sin(angle)
    step_angle = lax.broadcasted_iota(jnp.int32, (steps, HEAD), 0).astype(F32) * freq
    step_cos = jnp.cos(step_angle)
    step_sin = jnp.sin(step_angle)

    def step_turn(s):
        cosine = table[4, pl.ds(s, 1), :]
        sine = table[5, pl.ds(s, 1), :]
        return (
            cosine * step_cos - sine * step_sin,
            (sine * step_cos + cosine * step_sin) * sign,
        )

    def turn_queries(slot, s):
        cosine, sine = step_turn(s)
        stored = queries[slot].astype(F32)
        swapped = pltpu.roll(stored, HEAD // 2, 1)
        shape = (heads, steps, HEAD)
        turned = stored.reshape(shape) * cosine[None] + swapped.reshape(shape) * sine[None]
        return turned.reshape(rows, HEAD).astype(BF16)

    def contract(a, b, dims):
        return lax.dot_general(a, b, (dims, ((), ())), preferred_element_type=F32)

    def shifted(m):
        return m.astype(BF16).astype(F32)

    def partial(slot):
        s = owner_ref[slot]
        turned = turn_queries(slot, s)
        scores = contract(keys[s], turned, ((1,), (1,))) * score_scale
        tops, pieces = [], []
        for j in range(2):
            pieces.append(scores[j * BLOCK:(j + 1) * BLOCK])
            kept = live[j, pl.ds(s, 1), :] > 0.5
            tops.append((kept, jnp.where(kept, jnp.max(pieces[j], axis=0, keepdims=True), NEG)))
        m = shifted(jnp.maximum(tops[0][1], tops[1][1]))
        weights = [
            jnp.exp2(pieces[j] - jnp.where(tops[j][0], m, -NEG)) for j in range(2)
        ]
        l = jnp.sum(weights[0] + weights[1], axis=0, keepdims=True)
        weights = jnp.concatenate(weights, axis=0).astype(BF16)
        return m, l, contract(values[s], weights, ((0,), (0,)))

    sub8 = lax.broadcasted_iota(jnp.int32, (8, HEAD), 0)
    sub16 = lax.broadcasted_iota(jnp.int32, (16, HEAD), 0)

    def put(ref, m, l, o):
        ref[0:HEAD, :] = o
        ref[HEAD:HEAD + 8, :] = jnp.where(sub8 == 0, m, l)

    def get(ref):
        return ref[HEAD:HEAD + 1, :], ref[HEAD + 1:HEAD + 2, :], ref[0:HEAD, :]

    def put_half(ref, m, l, o):
        high = l.astype(BF16).astype(F32)
        ref[0:HEAD, :] = o.astype(BF16)
        tail = jnp.where(sub16 == 0, m, jnp.where(sub16 == 1, high, l - high))
        ref[HEAD:HEAD + 16, :] = tail.astype(BF16)

    def get_half(ref):
        tail = ref[HEAD:HEAD + 16, :].astype(F32)
        return tail[0:1], tail[1:2] + tail[2:3], ref[0:HEAD, :].astype(F32)

    def merge(parts):
        m = functools.reduce(jnp.maximum, [p[0] for p in parts])
        scales = [jnp.exp2(p[0] - m) for p in parts]
        l = functools.reduce(jnp.add, [p[1] * a for p, a in zip(parts, scales)])
        o = functools.reduce(jnp.add, [p[2] * a for p, a in zip(parts, scales)])
        return m, l, o

    def pair_copy(i):
        return remote(pair_out.at[i], pair_in.at[i], pair_send.at[i], pair_recv.at[i], dev(z, x, sib))

    def x_copy(i, d):
        return remote(x_out.at[i, d], x_in.at[i, d], x_send.at[i, d], x_recv.at[i, d],
                      dev(z, (x + d) % nx, c))

    def z_copy(i):
        return remote(z_out.at[i], z_in.at[i], z_send.at[i], z_recv.at[i], dev((z + far(i)) % nz, x, c))

    def stage_partials(i):
        z_ = (z + far(i)) % nz
        for d in range(nx):
            query_c_in(i, d).wait_recv()
        for d in range(nx):
            put(pair_out.at[i, d], *partial(dev(z_, (x + d) % nx, sib)))
        pair_copy(i).start()
        for d in range(nx):
            put(pair_own.at[i, d], *partial(dev(z_, (x + d) % nx, c)))

    def stage_x(i):
        pair_copy(i).wait_recv()
        for d in range(nx):
            merged = merge([get(pair_own.at[i, d]), get(pair_in.at[i, d])])
            if d == 0:
                put(x_own.at[i], *merged)
            else:
                put_half(x_out.at[i, d], *merged)
                x_copy(i, d).start()

    def stage_z(i):
        for d in range(1, nx):
            x_copy(i, d).wait_recv()
        merged = merge([get(x_own.at[i])] + [get_half(x_in.at[i, d]) for d in range(1, nx)])

        @pl.when(i < nz - 1)
        def _():
            put_half(z_out.at[i], *merged)
            z_copy(i).start()

        @pl.when(i == nz - 1)
        def _():
            put(z_own, *merged)

    forward_x(0)

    def step(i, carry):
        @pl.when(i < nz - 1)
        def _():
            forward_x(i + 1)

        @pl.when(i < nz)
        def _():
            stage_partials(i)

        @pl.when((i >= 1) & (i < nz + 1))
        def _():
            stage_x(i - 1)

        @pl.when(i >= 2)
        def _():
            stage_z(i - 2)

        return carry

    lax.fori_loop(0, nz + 2, step, 0)

    s = owner_ref[me]
    turned = turn_queries(me, s)
    cosine, sine = step_turn(s)
    fresh = newk_ref[...].astype(F32)
    fresh = (fresh * cosine + pltpu.roll(fresh, HEAD // 2, 1) * sine).astype(BF16)
    scores = contract(fresh, turned, ((1,), (1,))) * score_scale
    row_step = lax.broadcasted_iota(jnp.int32, (steps, rows), 1) % steps
    causal = lax.broadcasted_iota(jnp.int32, (steps, rows), 0) <= row_step
    scores = jnp.where(causal, scores, NEG)
    m = shifted(jnp.max(scores, axis=0, keepdims=True))
    weights = jnp.where(causal, jnp.exp2(scores - m), 0.0)
    l = jnp.sum(weights, axis=0, keepdims=True)
    parts = [(m, l, contract(newv_ref[...], weights.astype(BF16), ((0,), (0,))))]

    for i in range(nz - 1):
        z_copy(i).wait_recv()
        parts.append(get_half(z_in.at[i]))
    parts.append(get(z_own))
    m, l, o = merge(parts)
    result = jnp.transpose(o / l).astype(BF16)
    for g in range(heads):
        out_ref[:, g * HEAD:(g + 1) * HEAD] = result[g * steps:(g + 1) * steps]

    for r in range(1, group):
        counts_near(r).wait_send()
    for d in range(1, nz):
        counts_far(d).wait_send()
    for d in range(1, ny):
        remote(totals.at[tp], totals.at[tp], t_send.at[d], t_recv.at[d], me, (tp + d) % ny).wait_send()
    for i in range(nz):
        if i < nz - 1:
            query_z(i).wait_send()
            z_copy(i).wait_send()
        pair_copy(i).wait_send()
        for d in range(nx):
            query_c(i, d).wait_send()
            if d:
                query_x(i, d).wait_send()
                x_copy(i, d).wait_send()


def shards(
    nz, nx, ny,
    prompt_keys, prompt_values, keep_mask, owner_sequence, step_queries, new_keys, new_values,
):
    seqs = prompt_keys.shape[0]
    steps = step_queries.shape[1]
    flags = jnp.pad(keep_mask[:, :, 0].astype(F32).T, ((0, 0), (0, HEAD - seqs)))
    freq = frequencies(HEAD // 2)
    freq = jnp.concatenate([freq, freq])[None]
    any_spec = pl.BlockSpec(memory_space=pl.ANY)
    vmem = pl.BlockSpec(memory_space=pltpu.VMEM)
    dma = pltpu.SemaphoreType.DMA
    group = nx * 2
    out = pl.pallas_call(
        functools.partial(kernel, nz, nx, ny),
        out_shape=jax.ShapeDtypeStruct((steps, step_queries.shape[3]), BF16),
        in_specs=[pl.BlockSpec(memory_space=pltpu.SMEM)] + [vmem] * 5 + [any_spec] * 2,
        out_specs=vmem,
        scratch_shapes=[
            pltpu.VMEM((seqs, 2 * BLOCK, HEAD), BF16),
            pltpu.VMEM((seqs, 2 * BLOCK, HEAD), BF16),
            pltpu.VMEM((seqs, HEAD, HEAD), BF16),
            pltpu.VMEM((seqs, 1, HEAD), F32),
            pltpu.VMEM((ny, 1, HEAD), F32),
            pltpu.VMEM((6, seqs, HEAD), F32),
            pltpu.VMEM((2, seqs, HEAD), F32),
            pltpu.VMEM((nz, nx, HEAD + 8, HEAD), F32),
            pltpu.VMEM((nz, nx, HEAD + 8, HEAD), F32),
            pltpu.VMEM((nz, nx, HEAD + 8, HEAD), F32),
            pltpu.VMEM((nz, nx, HEAD + 16, HEAD), BF16),
            pltpu.VMEM((nz, nx, HEAD + 16, HEAD), BF16),
            pltpu.VMEM((nz, HEAD + 8, HEAD), F32),
            pltpu.VMEM((nz, HEAD + 16, HEAD), BF16),
            pltpu.VMEM((nz, HEAD + 16, HEAD), BF16),
            pltpu.VMEM((HEAD + 8, HEAD), F32),
            dma((2, nz)),
            dma((group,)), dma((group,)), dma((nz,)), dma((nz,)), dma((ny,)), dma((ny,)),
            dma((nz,)), dma((nz,)), dma((nz, nx)), dma((nz, nx)), dma((nz, nx)), dma((nz, nx)),
            dma((nz,)), dma((nz,)), dma((nz, nx)), dma((nz, nx)), dma((nz,)), dma((nz,)),
        ],
        compiler_params=pltpu.CompilerParams(
            collective_id=0, has_side_effects=True, vmem_limit_bytes=48 * 1024 * 1024
        ),
    )(
        owner_sequence, flags, freq, step_queries[0, :, 0], new_keys[0], new_values[0],
        prompt_keys, prompt_values,
    )
    return out[None, :, None]


def solution(mesh):
    in_specs = (
        P(None, "seq", "tp"),
        P(None, "seq", "tp"),
        P(None, "seq", "tp"),
        P(),
        P("seq", None, "tp", None),
        P("seq", None, "tp"),
        P("seq", None, "tp"),
    )
    out_specs = P("seq", None, "tp", None)
    seq = mesh.shape["seq"]
    nx = 4 if seq >= 64 else 2
    body = functools.partial(shards, seq // (2 * nx), nx, mesh.shape["tp"])
    return jax.shard_map(body, mesh=mesh, in_specs=in_specs, out_specs=out_specs, check_vma=False)
```

time: 258 us -> 63.3 us (0.25)
  blocking collectives: 113 us -> 0 us
  waiting for transfers between devices: 78.8 us -> 0 us
  Pallas kernels: 0 us -> 55.9 us
  starting transfers between devices: 20.3 us -> 0 us
  local copies, waits for them, and re-layouts: 22.2 us -> 5.6 us
  other arithmetic: 16.5 us -> 0.78 us
  matrix products: 4.57 us -> 0 us
    all_to_all x1 -> x0, blocking collectives: 105 us -> none  [shards(): lax.all_to_all(outgoing[0], 'seq', split_axis=0, concat_axis=0, tiled=True)]
    all_to_all x2 -> x0, waiting for transfers between devices: 78.8 us -> none  [the longest x1 78.8 us: shards(): lax.all_to_all(outgoing[1], 'seq', split_axis=0, concat_axis=0, tiled=True)]
    pallas_call x0 -> x1, Pallas kernels: none -> 55.9 us  [shards(): pl.pallas_call(functools.partial(kernel, nz, nx, ny), out_shape=jax.Shape...]
    all_to_all x2 -> x0, starting transfers between devices: 20.3 us -> none  [the longest x1 13 us: shards(): lax.all_to_all(outgoing[2], 'seq', split_axis=0, concat_axis=0, tiled=True)]
    gather x6 -> x0, local copies, waits for them, and re-layouts: 19.4 us -> none  [the longest x1 5.25 us: shards(): jnp.take(prompt_values, owner_sequence, axis=0)]
    pmax x1 -> x0, blocking collectives: 8.46 us -> none  [shards(): longest = lax.pmax(jnp.max(counts), 'tp')]
    select_n x3 -> x0, other arithmetic: 6.63 us -> none  [the longest x1 5.95 us: shards(): jnp.take(prompt_keys, owner_sequence, axis=0)]
    unnamed x8 -> x11, local copies, waits for them, and re-layouts: 0.8 us -> 5.59 us
  transfers between devices with their start and end apart: 2 -> 0, of which waited for: 1 -> 0; matrix products, arithmetic and copies ran while one was open for 9% -> 0% of each run, Pallas kernels for 0% -> 0%
where the time goes in v1:
time: 63.3 us; the launch traced here: 62.3 us
  Pallas kernels  55.9 us (88%)
  local copies, waits for them, and re-layouts  5.6 us (9%)
  other arithmetic  0.78 us (1%)
    pallas_call x1, Pallas kernels, shards(): pl.pallas_call(functools.partial(kernel, nz, nx, ny), out_shape=jax.Shape...  55.9 us
    unnamed x11, local copies, waits for them, and re-layouts  5.59 us

profile of v1, /device:TPU:1, one launch (start us, length us, event | category | flops | bytes accessed | tf_op | source)
XLA Modules:
  0.0 62.3 jit_solution(5323834930133445445)
XLA Ops:
  0.0 0.1 maximum_bitcast_fusion.freq_ref
  0.1 0.7 %convert_element_type.13 = f32[64,2,1]{0,2,1:T(1,128)S(1)} convert(s32[64,2,1]{0,2,1:T(1,128)} %param.9) | non-fusion elementwise | flops 128 | bytes 1024 | tf_op jit(solution)/shard_map/convert_element_type | solution.py:396
  0.8 0.0 copy-start
  0.8 2.2 %copy-done = bf16[64,256,128]{2,1,0:T(8,128)(2,1)S(1)} copy-done((bf16[64,256,128]{2,1,0:T(8,128)(2,1)S(1)}, bf16[64,256,128]{2,1,0:T(8,128)(2,1)}, u32[]{:S(2)}) %copy-start) | copy-done | bytes 4194328
  3.0 0.0 copy-start.1
  3.0 0.8 %copy-done.1 = bf16[1,16,1,1024]{3,1,2,0:T(8,128)(2,1)S(1)} copy-done((bf16[1,16,1,1024]{3,1,2,0:T(8,128)(2,1)S(1)}, bf16[1,16,1,1024]{3,1,2,0:T(8,128)(2,1)}, u32[]{:S(2)}) %copy-start.1) | copy-done | bytes 32792
  3.7 0.0 copy-start.2
  3.7 0.7 %copy-done.2 = bf16[1,16,128]{2,1,0:T(8,128)(2,1)S(1)} copy-done((bf16[1,16,128]{2,1,0:T(8,128)(2,1)S(1)}, bf16[1,16,128]{2,1,0:T(8,128)(2,1)}, u32[]{:S(2)}) %copy-start.2) | copy-done | bytes 4120
  4.4 0.0 copy-start.3
  4.4 0.7 %copy-done.3 = bf16[1,16,128]{2,1,0:T(8,128)(2,1)S(1)} copy-done((bf16[1,16,128]{2,1,0:T(8,128)(2,1)S(1)}, bf16[1,16,128]{2,1,0:T(8,128)(2,1)}, u32[]{:S(2)}) %copy-start.3) | copy-done | bytes 4120
  5.1 0.0 copy-start.4
  5.1 0.7 %copy-done.4 = s32[64]{0:T(128)S(1)} copy-done((s32[64]{0:T(128)S(1)}, s32[64]{0:T(128)}, u32[]{:S(2)}) %copy-start.4) | copy-done | bytes 280
  5.8 55.9 %shard_map.73 = bf16[16,1024]{1,0:T(8,128)(2,1)S(1)} custom-call(s32[64]{0:T(128)S(1)} %copy-done.4, f32[2,128]{1,0:T(2,128)S(1)} %pad.4.flags_ref, f32[1,128]{1,0:T(1,128)S(1)} %maximum_bitcast_fusion.freq_ref, bf16[16,1024]{1,0:T(8,128)(2,1)S(1)} %bitcast.10, bf16[16,128]{1,0:T(8,128)(2,1)S(1)} %bitcast.11, bf16[16,128]{1,0:T(8,128)(2,1)S(1)} %bitcast.12, ...), custom_call_target="tpu_custom_call" | custom-call | tf_op jit(solution)/shard_map/pallas_call | solution.py:403
  61.7 0.6 copy.9
  (2 shorter events, 0.0 us)
Async XLA Ops:
  0.8 2.2 %copy-start = (bf16[64,256,128]{2,1,0:T(8,128)(2,1)S(1)}, bf16[64,256,128]{2,1,0:T(8,128)(2,1)}, u32[]{:S(2)}) copy-start(bf16[64,256,128]{2,1,0:T(8,128)(2,1)} %keys_hbm.1) | copy-start | bytes 12582916
  3.0 0.8 %copy-start.1 = (bf16[1,16,1,1024]{3,1,2,0:T(8,128)(2,1)S(1)}, bf16[1,16,1,1024]{3,1,2,0:T(8,128)(2,1)}, u32[]{:S(2)}) copy-start(bf16[1,16,1,1024]{3,1,2,0:T(8,128)(2,1)} %param.11) | copy-start | bytes 98308
  3.7 0.7 %copy-start.2 = (bf16[1,16,128]{2,1,0:T(8,128)(2,1)S(1)}, bf16[1,16,128]{2,1,0:T(8,128)(2,1)}, u32[]{:S(2)}) copy-start(bf16[1,16,128]{2,1,0:T(8,128)(2,1)} %param.12) | copy-start | bytes 12292
  4.4 0.7 %copy-start.3 = (bf16[1,16,128]{2,1,0:T(8,128)(2,1)S(1)}, bf16[1,16,128]{2,1,0:T(8,128)(2,1)}, u32[]{:S(2)}) copy-start(bf16[1,16,128]{2,1,0:T(8,128)(2,1)} %param.13) | copy-start | bytes 12292
  5.1 0.7 %copy-start.4 = (s32[64]{0:T(128)S(1)}, s32[64]{0:T(128)}, u32[]{:S(2)}) copy-start(s32[64]{0:T(128)} %owner_ref.1) | copy-start | bytes 772

commit v2 on v1

--- a/solution.py
+++ b/solution.py
@@ -11,6 +11,7 @@
 BLOCK = 128
 HEAD = 128
 NEG = -1e30
+LAG = 4
 MESH = pl.DeviceIdType.MESH
 F32 = jnp.float32
 BF16 = jnp.bfloat16
@@ -29,13 +30,13 @@
 
 def kernel(
     nz, nx, ny,
-    owner_ref, flags_ref, freq_ref, query_ref, newk_ref, newv_ref, keys_hbm, values_hbm,
+    owner_hbm, mask_hbm, freq_ref, query_hbm, newk_hbm, newv_hbm, keys_hbm, values_hbm,
     out_ref,
+    owner_ref, mask_ref, query_ref, newk_ref, newv_ref,
     keys, values, queries, counts, totals, table, live, pair_out, pair_in, pair_own,
     x_out, x_in, x_own, z_out, z_in, z_own,
-    load_sem, c1_send, c1_recv, c2_send, c2_recv, t_send, t_recv,
-    qz_send, qz_recv, qx_send, qx_recv, qc_send, qc_recv,
-    pair_send, pair_recv, x_send, x_recv, z_send, z_recv,
+    load_sem, small_sem, send_sem, c1_recv, c2_recv, t_recv,
+    qz_recv, qx_recv, qc_recv, pair_recv, x_recv, z_recv,
 ):
     seqs = nz * nx * 2
     group = nx * 2
@@ -59,24 +60,40 @@
         half = nz // 2
         return (half + (i % 2) * (nz - (i + 1) // 2) + (1 - i % 2) * (i // 2)) % nz
 
-    def remote(src, dst, send, recv, where, where_tp=None):
+    def remote(ref, dst, send, recv, where, where_tp=None):
         return pltpu.make_async_remote_copy(
-            src_ref=src, dst_ref=dst, send_sem=send, recv_sem=recv,
+            src_ref=ref, dst_ref=dst, send_sem=send_sem.at[send], recv_sem=recv,
             device_id=(where, tp if where_tp is None else where_tp), device_id_type=MESH,
         )
 
-    chunk = seqs // nz
-
-    def load(i, which):
-        src, dst = ((keys_hbm, keys), (values_hbm, values))[which]
+    def drain(ref, sem):
+        pltpu.make_async_copy(ref, ref, sem).wait()
+
+    chunks = 4 if seqs > 8 else 2
+    chunk = seqs // chunks
+
+    def load(i):
         part = pl.ds(i * chunk, chunk)
-        return pltpu.make_async_copy(src.at[part], dst.at[part], load_sem.at[which, i])
-
-    for i in range(nz):
-        load(i, 0).start()
-        load(i, 1).start()
-
-    counts[me] = flags_ref[0:1, :] + flags_ref[1:2, :]
+        return pltpu.make_async_copy(keys_hbm.at[part], keys.at[part], load_sem.at[i])
+
+    load_values = pltpu.make_async_copy(values_hbm, values, load_sem.at[chunks])
+    small = [
+        pltpu.make_async_copy(src, dst, small_sem.at[i])
+        for i, (src, dst) in enumerate((
+            (mask_hbm, mask_ref), (query_hbm, query_ref), (owner_hbm, owner_ref),
+            (newk_hbm, newk_ref), (newv_hbm, newv_ref),
+        ))
+    ]
+    for copy in small:
+        copy.start()
+    for i in range(chunks):
+        load(i).start()
+    load_values.start()
+
+    small[0].wait()
+    flags = [mask_ref[j].astype(F32) for j in range(2)]
+    counts[me] = flags[0] + flags[1]
+    small[1].wait()
     for g in range(heads):
         queries[me, g * steps:(g + 1) * steps, :] = query_ref[:, g * HEAD:(g + 1) * HEAD]
 
@@ -92,46 +109,31 @@
     pl.semaphore_wait(barrier, group - 1 + nz - 1 + ny - 1)
 
     def counts_near(r):
-        return remote(counts.at[me], counts.at[me], c1_send.at[r], c1_recv.at[r], near + (xc + r) % group)
-
-    def counts_near_in(r):
-        slot = near + (xc - r + group) % group
-        return remote(counts.at[slot], counts.at[slot], c1_send.at[r], c1_recv.at[r], slot)
+        return remote(counts.at[me], counts.at[me], 0, c1_recv, near + (xc + r) % group)
 
     def counts_far(d):
-        part = pl.ds(z * group, group)
-        return remote(counts.at[part], counts.at[part], c2_send.at[d], c2_recv.at[d], dev((z + d) % nz, x, c))
-
-    def counts_far_in(d):
-        z_ = (z - d + nz) % nz
-        part = pl.ds(z_ * group, group)
-        return remote(counts.at[part], counts.at[part], c2_send.at[d], c2_recv.at[d], dev(z_, x, c))
+        part = pl.ds(near, group)
+        return remote(counts.at[part], counts.at[part], 1, c2_recv, dev((z + d) % nz, x, c))
+
+    def totals_out(d):
+        return remote(totals.at[tp], totals.at[tp], 2, t_recv, me, (tp + d) % ny)
+
+    def query(slot, recv, where):
+        return remote(queries.at[slot], queries.at[slot], 3, recv, where)
 
     def query_z(i):
-        return remote(queries.at[me], queries.at[me], qz_send.at[i], qz_recv.at[i],
-                      dev((z - far(i) + nz) % nz, x, c))
+        return query(me, qz_recv.at[i], dev((z - far(i) + nz) % nz, x, c))
 
     def query_z_in(i):
         slot = dev((z + far(i)) % nz, x, c)
-        return remote(queries.at[slot], queries.at[slot], qz_send.at[i], qz_recv.at[i], slot)
+        return query(slot, qz_recv.at[i], slot)
 
     def query_x(i, d):
-        slot = dev((z + far(i)) % nz, x, c)
-        return remote(queries.at[slot], queries.at[slot], qx_send.at[i, d], qx_recv.at[i, d],
-                      dev(z, (x + d) % nx, c))
-
-    def query_x_in(i, d):
-        x_ = (x - d + nx) % nx
-        slot = dev((z + far(i)) % nz, x_, c)
-        return remote(queries.at[slot], queries.at[slot], qx_send.at[i, d], qx_recv.at[i, d], dev(z, x_, c))
+        return query(dev((z + far(i)) % nz, x, c), qx_recv.at[i], dev(z, (x + d) % nx, c))
 
     def query_c(i, d):
         slot = dev((z + far(i)) % nz, (x - d + nx) % nx, c)
-        return remote(queries.at[slot], queries.at[slot], qc_send.at[i, d], qc_recv.at[i, d], dev(z, x, sib))
-
-    def query_c_in(i, d):
-        slot = dev((z + far(i)) % nz, (x - d + nx) % nx, sib)
-        return remote(queries.at[slot], queries.at[slot], qc_send.at[i, d], qc_recv.at[i, d], dev(z, x, sib))
+        return query(slot, qc_recv.at[i], dev(z, x, sib))
 
     def forward_z(i):
         for d in range(1, nx):
@@ -139,47 +141,48 @@
         query_c(i, 0).start()
 
     def forward_x(i):
+        drain(queries.at[pl.ds(0, nx - 1)], qx_recv.at[i])
         for d in range(1, nx):
-            query_x_in(i, d).wait_recv()
             query_c(i, d).start()
 
     for r in range(1, group):
         counts_near(r).start()
     for i in range(nz - 1):
         query_z(i).start()
-    for r in range(1, group):
-        counts_near_in(r).wait_recv()
+    forward_z(nz - 1)
+    drain(counts.at[pl.ds(0, group - 1)], c1_recv)
     for d in range(1, nz):
         counts_far(d).start()
-    forward_z(nz - 1)
-    for d in range(1, nz):
-        counts_far_in(d).wait_recv()
-
-    before = jnp.zeros((1, HEAD), F32)
-    total = jnp.zeros((1, HEAD), F32)
+    for i in range(nz - 1):
+        query_z_in(i).wait_recv()
+        forward_z(i)
+    drain(counts.at[pl.ds(0, (nz - 1) * group)], c2_recv)
+
+    before = jnp.zeros((1, seqs), F32)
+    total = jnp.zeros((1, seqs), F32)
     for j in range(seqs):
         row = counts[j]
         total = total + row
         before = before + jnp.where(j < me, row, 0.0)
     totals[tp] = total
     for d in range(1, ny):
-        remote(totals.at[tp], totals.at[tp], t_send.at[d], t_recv.at[d], me, (tp + d) % ny).start()
+        totals_out(d).start()
 
     freq = freq_ref[...]
     lane = lax.broadcasted_iota(jnp.int32, (1, HEAD), 1)
     sign = jnp.where(lane < HEAD // 2, -1.0, 1.0).astype(F32)
 
     def down(row):
-        return jnp.transpose(jnp.broadcast_to(row, (HEAD, HEAD)))[:seqs]
+        return jnp.transpose(jnp.broadcast_to(row, (HEAD, seqs)))
 
     slot0 = before
-    slot1 = before + flags_ref[0:1, :]
+    slot1 = before + flags[0]
     first_block = (2 * me).astype(F32)
     for j, slot in enumerate((slot0, slot1)):
         angle = (down(slot) - (first_block + j)) * float(BLOCK) * freq
         table[2 * j] = jnp.cos(angle)
         table[2 * j + 1] = jnp.sin(angle) * sign
-        live[j] = down(flags_ref[j:j + 1, :])
+        live[j] = down(flags[j])
 
     def rotate_keys(i, carry):
         for j in range(2):
@@ -191,19 +194,16 @@
             keys[i, part, :] = turned.astype(BF16)
         return carry
 
-    for i in range(nz):
-        load(i, 0).wait()
+    for i in range(chunks):
+        load(i).wait()
         lax.fori_loop(i * chunk, (i + 1) * chunk, rotate_keys, 0)
-        if i < nz - 1:
-            query_z_in(i).wait_recv()
-            forward_z(i)
-    for i in range(nz):
-        load(i, 1).wait()
+    load_values.wait()
+
+    for copy in small[2:]:
+        copy.wait()
 
     longest = total
-    for d in range(1, ny):
-        slot = (tp - d + ny) % ny
-        remote(totals.at[slot], totals.at[slot], t_send.at[d], t_recv.at[d], me, slot).wait_recv()
+    drain(totals.at[pl.ds(0, ny - 1)], t_recv)
     for d in range(1, ny):
         longest = jnp.maximum(longest, totals[(tp + d) % ny])
     angle = down(longest) * float(BLOCK) * freq
@@ -280,19 +280,18 @@
         return m, l, o
 
     def pair_copy(i):
-        return remote(pair_out.at[i], pair_in.at[i], pair_send.at[i], pair_recv.at[i], dev(z, x, sib))
+        return remote(pair_out.at[i], pair_in.at[i], 4, pair_recv.at[i], dev(z, x, sib))
 
     def x_copy(i, d):
-        return remote(x_out.at[i, d], x_in.at[i, d], x_send.at[i, d], x_recv.at[i, d],
+        return remote(x_out.at[i, d - 1], x_in.at[i, d - 1], 5, x_recv.at[i],
                       dev(z, (x + d) % nx, c))
 
     def z_copy(i):
-        return remote(z_out.at[i], z_in.at[i], z_send.at[i], z_recv.at[i], dev((z + far(i)) % nz, x, c))
+        return remote(z_out.at[i], z_in.at[i], 6, z_recv.at[i], dev((z + far(i)) % nz, x, c))
 
     def stage_partials(i):
         z_ = (z + far(i)) % nz
-        for d in range(nx):
-            query_c_in(i, d).wait_recv()
+        drain(queries.at[pl.ds(0, nx)], qc_recv.at[i])
         for d in range(nx):
             put(pair_out.at[i, d], *partial(dev(z_, (x + d) % nx, sib)))
         pair_copy(i).start()
@@ -306,13 +305,12 @@
             if d == 0:
                 put(x_own.at[i], *merged)
             else:
-                put_half(x_out.at[i, d], *merged)
+                put_half(x_out.at[i, d - 1], *merged)
                 x_copy(i, d).start()
 
     def stage_z(i):
-        for d in range(1, nx):
-            x_copy(i, d).wait_recv()
-        merged = merge([get(x_own.at[i])] + [get_half(x_in.at[i, d]) for d in range(1, nx)])
+        drain(x_in.at[i], x_recv.at[i])
+        merged = merge([get(x_own.at[i])] + [get_half(x_in.at[i, d]) for d in range(nx - 1)])
 
         @pl.when(i < nz - 1)
         def _():
@@ -334,17 +332,18 @@
         def _():
             stage_partials(i)
 
-        @pl.when((i >= 1) & (i < nz + 1))
+        @pl.when(i >= 1)
         def _():
             stage_x(i - 1)
 
-        @pl.when(i >= 2)
-        def _():
-            stage_z(i - 2)
+        @pl.when(i >= lag)
+        def _():
+            stage_z(i - lag)
 
         return carry
 
-    lax.fori_loop(0, nz + 2, step, 0)
+    lag = min(LAG, nz)
+    lax.fori_loop(0, nz + 1, step, 0)
 
     s = owner_ref[me]
     turned = turn_queries(me, s)
@@ -358,8 +357,14 @@
     m = shifted(jnp.max(scores, axis=0, keepdims=True))
     weights = jnp.where(causal, jnp.exp2(scores - m), 0.0)
     l = jnp.sum(weights, axis=0, keepdims=True)
-    parts = [(m, l, contract(newv_ref[...], weights.astype(BF16), ((0,), (0,))))]
-
+    fresh = (m, l, contract(newv_ref[...], weights.astype(BF16), ((0,), (0,))))
+
+    def trail(i, carry):
+        stage_z(i)
+        return carry
+
+    lax.fori_loop(nz + 1 - lag, nz, trail, 0)
+    parts = [fresh]
     for i in range(nz - 1):
         z_copy(i).wait_recv()
         parts.append(get_half(z_in.at[i]))
@@ -369,22 +374,11 @@
     for g in range(heads):
         out_ref[:, g * HEAD:(g + 1) * HEAD] = result[g * steps:(g + 1) * steps]
 
-    for r in range(1, group):
-        counts_near(r).wait_send()
-    for d in range(1, nz):
-        counts_far(d).wait_send()
-    for d in range(1, ny):
-        remote(totals.at[tp], totals.at[tp], t_send.at[d], t_recv.at[d], me, (tp + d) % ny).wait_send()
-    for i in range(nz):
-        if i < nz - 1:
-            query_z(i).wait_send()
-            z_copy(i).wait_send()
-        pair_copy(i).wait_send()
-        for d in range(nx):
-            query_c(i, d).wait_send()
-            if d:
-                query_x(i, d).wait_send()
-                x_copy(i, d).wait_send()
+    for kind, ref in enumerate((
+        counts.at[pl.ds(0, group - 1)], counts.at[pl.ds(0, (nz - 1) * group)], totals.at[pl.ds(0, ny - 1)],
+        queries.at[pl.ds(0, seqs - 1)], pair_out, x_out, z_out,
+    )):
+        drain(ref, send_sem.at[kind])
 
 
 def shards(
@@ -393,45 +387,48 @@
 ):
     seqs = prompt_keys.shape[0]
     steps = step_queries.shape[1]
-    flags = jnp.pad(keep_mask[:, :, 0].astype(F32).T, ((0, 0), (0, HEAD - seqs)))
     freq = frequencies(HEAD // 2)
     freq = jnp.concatenate([freq, freq])[None]
-    any_spec = pl.BlockSpec(memory_space=pl.ANY)
+    hbm = pl.BlockSpec(memory_space=pltpu.HBM)
     vmem = pl.BlockSpec(memory_space=pltpu.VMEM)
     dma = pltpu.SemaphoreType.DMA
     group = nx * 2
     out = pl.pallas_call(
         functools.partial(kernel, nz, nx, ny),
         out_shape=jax.ShapeDtypeStruct((steps, step_queries.shape[3]), BF16),
-        in_specs=[pl.BlockSpec(memory_space=pltpu.SMEM)] + [vmem] * 5 + [any_spec] * 2,
+        in_specs=[hbm, hbm, vmem] + [hbm] * 5,
         out_specs=vmem,
         scratch_shapes=[
+            pltpu.SMEM((seqs,), jnp.int32),
+            pltpu.VMEM((2, 1, seqs), jnp.int32),
+            pltpu.VMEM((steps, step_queries.shape[3]), BF16),
+            pltpu.VMEM((steps, HEAD), BF16),
+            pltpu.VMEM((steps, HEAD), BF16),
             pltpu.VMEM((seqs, 2 * BLOCK, HEAD), BF16),
             pltpu.VMEM((seqs, 2 * BLOCK, HEAD), BF16),
             pltpu.VMEM((seqs, HEAD, HEAD), BF16),
-            pltpu.VMEM((seqs, 1, HEAD), F32),
-            pltpu.VMEM((ny, 1, HEAD), F32),
+            pltpu.VMEM((seqs, 1, seqs), F32),
+            pltpu.VMEM((ny, 1, seqs), F32),
             pltpu.VMEM((6, seqs, HEAD), F32),
             pltpu.VMEM((2, seqs, HEAD), F32),
             pltpu.VMEM((nz, nx, HEAD + 8, HEAD), F32),
             pltpu.VMEM((nz, nx, HEAD + 8, HEAD), F32),
             pltpu.VMEM((nz, nx, HEAD + 8, HEAD), F32),
-            pltpu.VMEM((nz, nx, HEAD + 16, HEAD), BF16),
-            pltpu.VMEM((nz, nx, HEAD + 16, HEAD), BF16),
+            pltpu.VMEM((nz, nx - 1, HEAD + 16, HEAD), BF16),
+            pltpu.VMEM((nz, nx - 1, HEAD + 16, HEAD), BF16),
             pltpu.VMEM((nz, HEAD + 8, HEAD), F32),
-            pltpu.VMEM((nz, HEAD + 16, HEAD), BF16),
-            pltpu.VMEM((nz, HEAD + 16, HEAD), BF16),
+            pltpu.VMEM((nz - 1, HEAD + 16, HEAD), BF16),
+            pltpu.VMEM((nz - 1, HEAD + 16, HEAD), BF16),
             pltpu.VMEM((HEAD + 8, HEAD), F32),
-            dma((2, nz)),
-            dma((group,)), dma((group,)), dma((nz,)), dma((nz,)), dma((ny,)), dma((ny,)),
-            dma((nz,)), dma((nz,)), dma((nz, nx)), dma((nz, nx)), dma((nz, nx)), dma((nz, nx)),
-            dma((nz,)), dma((nz,)), dma((nz, nx)), dma((nz, nx)), dma((nz,)), dma((nz,)),
+            dma((5,)), dma((5,)), dma((7,)), dma, dma, dma,
+            dma((nz,)), dma((nz,)), dma((nz,)), dma((nz,)), dma((nz,)), dma((nz,)),
         ],
         compiler_params=pltpu.CompilerParams(
-            collective_id=0, has_side_effects=True, vmem_limit_bytes=48 * 1024 * 1024
+            collective_id=0, has_side_effects=True, vmem_limit_bytes=64 * 1024 * 1024
         ),
     )(
-        owner_sequence, flags, freq, step_queries[0, :, 0], new_keys[0], new_values[0],
+        owner_sequence, keep_mask.transpose(1, 2, 0), freq, step_queries[0, :, 0], new_keys[0],
+        new_values[0],
         prompt_keys, prompt_values,
     )
     return out[None, :, None]

time: 63.3 us -> 50.6 us (0.80); the launches traced: 62.3 us -> 50.5 us
  Pallas kernels: 55.9 us -> 48.5 us
  local copies, waits for them, and re-layouts: 5.6 us -> 1.38 us
    pallas_call x1, Pallas kernels: 55.9 us -> 48.5 us  [shards(): pl.pallas_call(functools.partial(kernel, nz, nx, ny), out_shape=jax.Shape...]
    unnamed x11 -> x1, local copies, waits for them, and re-layouts: 5.59 us -> 1.38 us
    convert_element_type x1 -> x0, other arithmetic: 0.69 us -> none  [shards(): keep_mask[:, :, 0].astype(F32)]
where the time goes in v2:
time: 50.6 us; the launch traced here: 50.5 us
  Pallas kernels  48.5 us (96%)
  local copies, waits for them, and re-layouts  1.38 us (3%)
  other arithmetic  0.61 us (1%)
    pallas_call x1, Pallas kernels, shards(): pl.pallas_call(functools.partial(kernel, nz, nx, ny), out_shape=jax.Shape...  48.5 us
    unnamed x1, local copies, waits for them, and re-layouts  1.38 us

profile of v2, /device:TPU:1, one launch (start us, length us, event | category | flops | bytes accessed | tf_op | source)
XLA Modules:
  0.0 50.5 jit_solution(6999128578825930991)
XLA Ops:
  0.0 0.6 %maximum_bitcast_fusion.freq_ref = f32[1,128]{1,0:T(1,128)} fusion(f32[64]{0:T(128)S(1)} %compare_select_fusion.1), kind=kLoop, calls=%fused_computation.2 | loop fusion | flops 128 | bytes 768 | tf_op jit(solution)/shard_map/broadcast_in_dim | solution.py:391
  0.6 48.5 %shard_map.73 = bf16[16,1024]{1,0:T(8,128)(2,1)} custom-call(s32[64]{0:T(128)} %owner_hbm.1, s32[2,1,64]{2,1,0:T(1,128)} %bitcast.11, f32[1,128]{1,0:T(1,128)} %maximum_bitcast_fusion.freq_ref, bf16[16,1024]{1,0:T(8,128)(2,1)} %bitcast.8, bf16[16,128]{1,0:T(8,128)(2,1)} %bitcast.9, bf16[16,128]{1,0:T(8,128)(2,1)} %bitcast.10, ...), custom_call_target="tpu_custom_call" | custom-call | tf_op jit(solution)/shard_map/pallas_call | solution.py:396
  49.1 1.4 %copy.9 = bf16[1,16,1,1024]{3,1,2,0:T(8,128)(2,1)} copy(bf16[1,16,1,1024]{3,1,2,0:T(8,128)(2,1)} %bitcast.7) | data formatting | bytes 65536
  (1 shorter events, 0.0 us)

commit v3 on v2

--- a/solution.py
+++ b/solution.py
@@ -34,7 +34,7 @@
     out_ref,
     owner_ref, mask_ref, query_ref, newk_ref, newv_ref,
     keys, values, queries, counts, totals, table, live, pair_out, pair_in, pair_own,
-    x_out, x_in, x_own, z_out, z_in, z_own,
+    x_out, x_in, x_own, z_out, z_in,
     load_sem, small_sem, send_sem, c1_recv, c2_recv, t_recv,
     qz_recv, qx_recv, qc_recv, pair_recv, x_recv, z_recv,
 ):
@@ -184,19 +184,20 @@
         table[2 * j + 1] = jnp.sin(angle) * sign
         live[j] = down(flags[j])
 
-    def rotate_keys(i, carry):
-        for j in range(2):
+    def rotate_keys(k, carry):
+        for i, j in ((2 * k, 0), (2 * k, 1), (2 * k + 1, 0), (2 * k + 1, 1)):
             cosine = table[2 * j, pl.ds(i, 1), :]
             sine = table[2 * j + 1, pl.ds(i, 1), :]
             part = pl.ds(j * BLOCK, BLOCK)
-            stored = keys[i, part, :].astype(F32)
-            turned = stored * cosine + pltpu.roll(stored, HEAD // 2, 1) * sine
+            packed = keys[i, part, :]
+            swapped = pltpu.roll(packed, HEAD // 2, 1).astype(F32)
+            turned = packed.astype(F32) * cosine + swapped * sine
             keys[i, part, :] = turned.astype(BF16)
         return carry
 
     for i in range(chunks):
         load(i).wait()
-        lax.fori_loop(i * chunk, (i + 1) * chunk, rotate_keys, 0)
+        lax.fori_loop(i * chunk // 2, (i + 1) * chunk // 2, rotate_keys, 0)
     load_values.wait()
 
     for copy in small[2:]:
@@ -235,25 +236,29 @@
     def shifted(m):
         return m.astype(BF16).astype(F32)
 
-    def partial(slot):
-        s = owner_ref[slot]
-        turned = turn_queries(slot, s)
-        scores = contract(keys[s], turned, ((1,), (1,))) * score_scale
-        tops, pieces = [], []
-        for j in range(2):
-            pieces.append(scores[j * BLOCK:(j + 1) * BLOCK])
-            kept = live[j, pl.ds(s, 1), :] > 0.5
-            tops.append((kept, jnp.where(kept, jnp.max(pieces[j], axis=0, keepdims=True), NEG)))
-        m = shifted(jnp.maximum(tops[0][1], tops[1][1]))
+    def partials(slots):
+        places = [owner_ref[slot] for slot in slots]
+        turned = [turn_queries(slot, s) for slot, s in zip(slots, places)]
+        scores = [contract(keys[s], q, ((1,), (1,))) * score_scale for s, q in zip(places, turned)]
+        kept = [[live[j, pl.ds(s, 1), :] > 0.5 for j in range(2)] for s in places]
+        pieces = [[a[j * BLOCK:(j + 1) * BLOCK] for j in range(2)] for a in scores]
+        tops = [
+            [jnp.where(k[j], jnp.max(a[j], axis=0, keepdims=True), NEG) for j in range(2)]
+            for k, a in zip(kept, pieces)
+        ]
+        m = [shifted(jnp.maximum(*t)) for t in tops]
         weights = [
-            jnp.exp2(pieces[j] - jnp.where(tops[j][0], m, -NEG)) for j in range(2)
+            [jnp.exp2(a[j] - jnp.where(k[j], b, -NEG)) for j in range(2)]
+            for k, a, b in zip(kept, pieces, m)
         ]
-        l = jnp.sum(weights[0] + weights[1], axis=0, keepdims=True)
-        weights = jnp.concatenate(weights, axis=0).astype(BF16)
-        return m, l, contract(values[s], weights, ((0,), (0,)))
+        l = [jnp.sum(w[0] + w[1], axis=0, keepdims=True) for w in weights]
+        o = [
+            contract(values[s], jnp.concatenate(w, axis=0).astype(BF16), ((0,), (0,)))
+            for s, w in zip(places, weights)
+        ]
+        return list(zip(m, l, o))
 
     sub8 = lax.broadcasted_iota(jnp.int32, (8, HEAD), 0)
-    sub16 = lax.broadcasted_iota(jnp.int32, (16, HEAD), 0)
 
     def put(ref, m, l, o):
         ref[0:HEAD, :] = o
@@ -265,11 +270,11 @@
     def put_half(ref, m, l, o):
         high = l.astype(BF16).astype(F32)
         ref[0:HEAD, :] = o.astype(BF16)
-        tail = jnp.where(sub16 == 0, m, jnp.where(sub16 == 1, high, l - high))
-        ref[HEAD:HEAD + 16, :] = tail.astype(BF16)
+        tail = jnp.where(sub8 == 0, m, jnp.where(sub8 == 1, high, l - high))
+        ref[HEAD:HEAD + 8, :] = tail.astype(BF16)
 
     def get_half(ref):
-        tail = ref[HEAD:HEAD + 16, :].astype(F32)
+        tail = ref[HEAD:HEAD + 8, :].astype(F32)
         return tail[0:1], tail[1:2] + tail[2:3], ref[0:HEAD, :].astype(F32)
 
     def merge(parts):
@@ -292,11 +297,11 @@
     def stage_partials(i):
         z_ = (z + far(i)) % nz
         drain(queries.at[pl.ds(0, nx)], qc_recv.at[i])
-        for d in range(nx):
-            put(pair_out.at[i, d], *partial(dev(z_, (x + d) % nx, sib)))
+        for d, part in enumerate(partials([dev(z_, (x + d) % nx, sib) for d in range(nx)])):
+            put(pair_out.at[i, d], *part)
         pair_copy(i).start()
-        for d in range(nx):
-            put(pair_own.at[i, d], *partial(dev(z_, (x + d) % nx, c)))
+        for d, part in enumerate(partials([dev(z_, (x + d) % nx, c) for d in range(nx)])):
+            put(pair_own.at[i, d], *part)
 
     def stage_x(i):
         pair_copy(i).wait_recv()
@@ -310,16 +315,11 @@
 
     def stage_z(i):
         drain(x_in.at[i], x_recv.at[i])
-        merged = merge([get(x_own.at[i])] + [get_half(x_in.at[i, d]) for d in range(nx - 1)])
-
-        @pl.when(i < nz - 1)
-        def _():
-            put_half(z_out.at[i], *merged)
-            z_copy(i).start()
-
-        @pl.when(i == nz - 1)
-        def _():
-            put(z_own, *merged)
+        return merge([get(x_own.at[i])] + [get_half(x_in.at[i, d]) for d in range(nx - 1)])
+
+    def send_z(i):
+        put_half(z_out.at[i], *stage_z(i))
+        z_copy(i).start()
 
     forward_x(0)
 
@@ -336,9 +336,9 @@
         def _():
             stage_x(i - 1)
 
-        @pl.when(i >= lag)
+        @pl.when((i >= lag) & (i - lag < nz - 1))
         def _():
-            stage_z(i - lag)
+            send_z(i - lag)
 
         return carry
 
@@ -359,16 +359,13 @@
     l = jnp.sum(weights, axis=0, keepdims=True)
     fresh = (m, l, contract(newv_ref[...], weights.astype(BF16), ((0,), (0,))))
 
-    def trail(i, carry):
-        stage_z(i)
-        return carry
-
-    lax.fori_loop(nz + 1 - lag, nz, trail, 0)
+    for i in range(nz + 1 - lag, nz - 1):
+        send_z(i)
     parts = [fresh]
-    for i in range(nz - 1):
+    parts.append(stage_z(nz - 1))
+    for i in range(nz-1):
         z_copy(i).wait_recv()
         parts.append(get_half(z_in.at[i]))
-    parts.append(get(z_own))
     m, l, o = merge(parts)
     result = jnp.transpose(o / l).astype(BF16)
     for g in range(heads):
@@ -414,12 +411,11 @@
             pltpu.VMEM((nz, nx, HEAD + 8, HEAD), F32),
             pltpu.VMEM((nz, nx, HEAD + 8, HEAD), F32),
             pltpu.VMEM((nz, nx, HEAD + 8, HEAD), F32),
-            pltpu.VMEM((nz, nx - 1, HEAD + 16, HEAD), BF16),
-            pltpu.VMEM((nz, nx - 1, HEAD + 16, HEAD), BF16),
+            pltpu.VMEM((nz, nx - 1, HEAD + 8, HEAD), BF16),
+            pltpu.VMEM((nz, nx - 1, HEAD + 8, HEAD), BF16),
             pltpu.VMEM((nz, HEAD + 8, HEAD), F32),
-            pltpu.VMEM((nz - 1, HEAD + 16, HEAD), BF16),
-            pltpu.VMEM((nz - 1, HEAD + 16, HEAD), BF16),
-            pltpu.VMEM((HEAD + 8, HEAD), F32),
+            pltpu.VMEM((nz - 1, HEAD + 8, HEAD), BF16),
+            pltpu.VMEM((nz - 1, HEAD + 8, HEAD), BF16),
             dma((5,)), dma((5,)), dma((7,)), dma, dma, dma,
             dma((nz,)), dma((nz,)), dma((nz,)), dma((nz,)), dma((nz,)), dma((nz,)),
         ],

time: 50.6 us -> 47.2 us (0.933)
  Pallas kernels: 48.5 us -> 45.1 us
    pallas_call x1, Pallas kernels: 48.5 us -> 45.1 us  [shards(): pl.pallas_call(functools.partial(kernel, nz, nx, ny), out_shape=jax.Shape...]
where the time goes in v3:
time: 47.2 us; the launch traced here: 47.1 us
  Pallas kernels  45.1 us (96%)
  local copies, waits for them, and re-layouts  1.38 us (3%)
  other arithmetic  0.61 us (1%)
    pallas_call x1, Pallas kernels, shards(): pl.pallas_call(functools.partial(kernel, nz, nx, ny), out_shape=jax.Shape...  45.1 us
    unnamed x1, local copies, waits for them, and re-layouts  1.38 us

profile of v3, /device:TPU:1, one launch (start us, length us, event | category | flops | bytes accessed | tf_op | source)
XLA Modules:
  0.0 47.1 jit_solution(6151968565000135589)
XLA Ops:
  0.0 0.6 %maximum_bitcast_fusion.freq_ref = f32[1,128]{1,0:T(1,128)} fusion(f32[64]{0:T(128)S(1)} %compare_select_fusion.1), kind=kLoop, calls=%fused_computation.2 | loop fusion | flops 128 | bytes 768 | tf_op jit(solution)/shard_map/broadcast_in_dim | solution.py:388
  0.6 45.1 %shard_map.73 = bf16[16,1024]{1,0:T(8,128)(2,1)} custom-call(s32[64]{0:T(128)} %owner_hbm.1, s32[2,1,64]{2,1,0:T(1,128)} %bitcast.11, f32[1,128]{1,0:T(1,128)} %maximum_bitcast_fusion.freq_ref, bf16[16,1024]{1,0:T(8,128)(2,1)} %bitcast.8, bf16[16,128]{1,0:T(8,128)(2,1)} %bitcast.9, bf16[16,128]{1,0:T(8,128)(2,1)} %bitcast.10, ...), custom_call_target="tpu_custom_call" | custom-call | tf_op jit(solution)/shard_map/pallas_call | solution.py:393
  45.7 1.4 %copy.9 = bf16[1,16,1,1024]{3,1,2,0:T(8,128)(2,1)} copy(bf16[1,16,1,1024]{3,1,2,0:T(8,128)(2,1)} %bitcast.7) | data formatting | bytes 65536
  (1 shorter events, 0.0 us)

commit v4 on v3

--- a/solution.py
+++ b/solution.py
@@ -300,6 +300,11 @@
         for d, part in enumerate(partials([dev(z_, (x + d) % nx, sib) for d in range(nx)])):
             put(pair_out.at[i, d], *part)
         pair_copy(i).start()
+
+        @pl.when(i >= 1)
+        def _():
+            stage_x(i - 1)
+
         for d, part in enumerate(partials([dev(z_, (x + d) % nx, c) for d in range(nx)])):
             put(pair_own.at[i, d], *part)
 
@@ -322,17 +327,18 @@
         z_copy(i).start()
 
     forward_x(0)
+    forward_x(1)
 
     def step(i, carry):
-        @pl.when(i < nz - 1)
+        @pl.when(i < nz - 2)
         def _():
-            forward_x(i + 1)
+            forward_x(i + 2)
 
         @pl.when(i < nz)
         def _():
             stage_partials(i)
 
-        @pl.when(i >= 1)
+        @pl.when(i == nz)
         def _():
             stage_x(i - 1)
 

time: 47.2 us -> 46.6 us (0.987)
  Pallas kernels: 45.1 us -> 44.4 us
    pallas_call x1, Pallas kernels: 45.1 us -> 44.4 us  [shards(): pl.pallas_call(functools.partial(kernel, nz, nx, ny), out_shape=jax.Shape...]
where the time goes in v4:
time: 46.6 us; the launch traced here: 46.4 us
  Pallas kernels  44.4 us (95%)
  local copies, waits for them, and re-layouts  1.38 us (3%)
  other arithmetic  0.61 us (1%)
    pallas_call x1, Pallas kernels, shards(): pl.pallas_call(functools.partial(kernel, nz, nx, ny), out_shape=jax.Shape...  44.4 us
    unnamed x1, local copies, waits for them, and re-layouts  1.38 us

profile of v4, /device:TPU:1, one launch (start us, length us, event | category | flops | bytes accessed | tf_op | source)
XLA Modules:
  0.0 46.4 jit_solution(18325875414389815875)
XLA Ops:
  0.0 0.6 %maximum_bitcast_fusion.freq_ref = f32[1,128]{1,0:T(1,128)} fusion(f32[64]{0:T(128)S(1)} %compare_select_fusion.1), kind=kLoop, calls=%fused_computation.2 | loop fusion | flops 128 | bytes 768 | tf_op jit(solution)/shard_map/broadcast_in_dim | solution.py:394
  0.6 44.4 %shard_map.73 = bf16[16,1024]{1,0:T(8,128)(2,1)} custom-call(s32[64]{0:T(128)} %owner_hbm.1, s32[2,1,64]{2,1,0:T(1,128)} %bitcast.11, f32[1,128]{1,0:T(1,128)} %maximum_bitcast_fusion.freq_ref, bf16[16,1024]{1,0:T(8,128)(2,1)} %bitcast.8, bf16[16,128]{1,0:T(8,128)(2,1)} %bitcast.9, bf16[16,128]{1,0:T(8,128)(2,1)} %bitcast.10, ...), custom_call_target="tpu_custom_call" | custom-call | tf_op jit(solution)/shard_map/pallas_call | solution.py:399
  45.1 1.4 %copy.9 = bf16[1,16,1,1024]{3,1,2,0:T(8,128)(2,1)} copy(bf16[1,16,1,1024]{3,1,2,0:T(8,128)(2,1)} %bitcast.7) | data formatting | bytes 65536
  (1 shorter events, 0.0 us)

commit v5 on v4

--- a/solution.py
+++ b/solution.py
@@ -259,22 +259,24 @@
         return list(zip(m, l, o))
 
     sub8 = lax.broadcasted_iota(jnp.int32, (8, HEAD), 0)
+    sub16 = lax.broadcasted_iota(jnp.int32, (16, HEAD), 0)
 
     def put(ref, m, l, o):
         ref[0:HEAD, :] = o
         ref[HEAD:HEAD + 8, :] = jnp.where(sub8 == 0, m, l)
 
     def get(ref):
-        return ref[HEAD:HEAD + 1, :], ref[HEAD + 1:HEAD + 2, :], ref[0:HEAD, :]
+        tail = ref[HEAD:HEAD + 8, :]
+        return tail[0:1], tail[1:2], ref[0:HEAD, :]
 
     def put_half(ref, m, l, o):
         high = l.astype(BF16).astype(F32)
         ref[0:HEAD, :] = o.astype(BF16)
-        tail = jnp.where(sub8 == 0, m, jnp.where(sub8 == 1, high, l - high))
-        ref[HEAD:HEAD + 8, :] = tail.astype(BF16)
+        tail = jnp.where(sub16 == 0, m, jnp.where(sub16 == 1, high, l - high))
+        ref[HEAD:HEAD + 16, :] = tail.astype(BF16)
 
     def get_half(ref):
-        tail = ref[HEAD:HEAD + 8, :].astype(F32)
+        tail = ref[HEAD:HEAD + 16, :].astype(F32)
         return tail[0:1], tail[1:2] + tail[2:3], ref[0:HEAD, :].astype(F32)
 
     def merge(parts):
@@ -410,18 +412,18 @@
             pltpu.VMEM((seqs, 2 * BLOCK, HEAD), BF16),
             pltpu.VMEM((seqs, 2 * BLOCK, HEAD), BF16),
             pltpu.VMEM((seqs, HEAD, HEAD), BF16),
-            pltpu.VMEM((seqs, 1, seqs), F32),
-            pltpu.VMEM((ny, 1, seqs), F32),
-            pltpu.VMEM((6, seqs, HEAD), F32),
-            pltpu.VMEM((2, seqs, HEAD), F32),
+            pltpu.VMEM((seqs + 8, 1, seqs), F32),
+            pltpu.VMEM((ny + 8, 1, seqs), F32),
+            pltpu.VMEM((7, seqs, HEAD), F32),
+            pltpu.VMEM((3, seqs, HEAD), F32),
             pltpu.VMEM((nz, nx, HEAD + 8, HEAD), F32),
             pltpu.VMEM((nz, nx, HEAD + 8, HEAD), F32),
             pltpu.VMEM((nz, nx, HEAD + 8, HEAD), F32),
-            pltpu.VMEM((nz, nx - 1, HEAD + 8, HEAD), BF16),
-            pltpu.VMEM((nz, nx - 1, HEAD + 8, HEAD), BF16),
+            pltpu.VMEM((nz, nx - 1, HEAD + 16, HEAD), BF16),
+            pltpu.VMEM((nz, nx - 1, HEAD + 16, HEAD), BF16),
             pltpu.VMEM((nz, HEAD + 8, HEAD), F32),
-            pltpu.VMEM((nz - 1, HEAD + 8, HEAD), BF16),
-            pltpu.VMEM((nz - 1, HEAD + 8, HEAD), BF16),
+            pltpu.VMEM((nz - 1, HEAD + 16, HEAD), BF16),
+            pltpu.VMEM((nz - 1, HEAD + 16, HEAD), BF16),
             dma((5,)), dma((5,)), dma((7,)), dma, dma, dma,
             dma((nz,)), dma((nz,)), dma((nz,)), dma((nz,)), dma((nz,)), dma((nz,)),
         ],

time: 46.6 us -> 47.2 us (1.013)
  Pallas kernels: 44.4 us -> 45.1 us
    pallas_call x1, Pallas kernels: 44.4 us -> 45.1 us  [shards(): pl.pallas_call(functools.partial(kernel, nz, nx, ny), out_shape=jax.Shape...]
where the time goes in v5:
time: 47.2 us; the launch traced here: 47.1 us
  Pallas kernels  45.1 us (96%)
  local copies, waits for them, and re-layouts  1.38 us (3%)
  other arithmetic  0.61 us (1%)
    pallas_call x1, Pallas kernels, shards(): pl.pallas_call(functools.partial(kernel, nz, nx, ny), out_shape=jax.Shape...  45.1 us
    unnamed x1, local copies, waits for them, and re-layouts  1.38 us

profile of v5, /device:TPU:1, one launch (start us, length us, event | category | flops | bytes accessed | tf_op | source)
XLA Modules:
  0.0 47.1 jit_solution(12060994231122824789)
XLA Ops:
  0.0 0.6 %maximum_bitcast_fusion.freq_ref = f32[1,128]{1,0:T(1,128)} fusion(f32[64]{0:T(128)S(1)} %compare_select_fusion.1), kind=kLoop, calls=%fused_computation.2 | loop fusion | flops 128 | bytes 768 | tf_op jit(solution)/shard_map/broadcast_in_dim | solution.py:396
  0.6 45.1 %shard_map.73 = bf16[16,1024]{1,0:T(8,128)(2,1)} custom-call(s32[64]{0:T(128)} %owner_hbm.1, s32[2,1,64]{2,1,0:T(1,128)} %bitcast.11, f32[1,128]{1,0:T(1,128)} %maximum_bitcast_fusion.freq_ref, bf16[16,1024]{1,0:T(8,128)(2,1)} %bitcast.8, bf16[16,128]{1,0:T(8,128)(2,1)} %bitcast.9, bf16[16,128]{1,0:T(8,128)(2,1)} %bitcast.10, ...), custom_call_target="tpu_custom_call" | custom-call | tf_op jit(solution)/shard_map/pallas_call | solution.py:401
  45.7 1.4 %copy.9 = bf16[1,16,1,1024]{3,1,2,0:T(8,128)(2,1)} copy(bf16[1,16,1,1024]{3,1,2,0:T(8,128)(2,1)} %bitcast.7) | data formatting | bytes 65536
  (1 shorter events, 0.0 us)
